TPU v7x, 256 devices: a whole 4x4x8 slice. The times are simulated.
256 devices in a mesh: dp: 4 (over z_lo), expert: 64 (over z_hi, y, x, core).
Axes of the slice: x: 4, y: 4, z: 8 (z_hi: 2, z_lo: 4; z = z_hi * 4 + z_lo), core: 2. Of those that a mesh axis runs over, the one named last changes fastest.
Arguments:
- hidden: bfloat16 [262144, 768], P(('dp', 'expert')), may hold values from -6 to 6
- grad_out: bfloat16 [262144, 2048], P(('dp', 'expert')), may hold values from -0.19921875 to 0.19921875
- block_slot: int32 [256, 8], P(('dp', 'expert')), may hold values from 0 to 2, as said below
- block_count: int32 [256], P(('dp', 'expert')), may hold values from 2 to 8, as said below
- replica_expert: int32 [64], replicated, may hold values from 0 to 127, as said below
Outputs:
- grad_down: bfloat16 [128, 768, 2048], P('expert', None, 'dp')
Inputs may be any that keep to these rules, and one draw needn't show every extreme that they name: `replica_expert`: Expert-axis index k is home to experts k * 2 to k * 2 + 1 and has one replica slot. The indices holding an expert homed at h are h alone, or h and (h + 32) mod 64, or h and (h + m * 16) mod 64 for m = 1, 2, 3; in every draw some expert homed at index 63 has such a set of four. `block_count`: some device has all 8 blocks live. `block_slot`: block 0 of every device belongs to the replica slot 2.
All inputs are finite; a program needn't handle non-finite values.
Results may differ from a plain program's by a relative error of at most 0.0065.
Values may be sent and summed in bfloat16 or wider, within the bound.
A program may use at most 128 MiB of HBM per device.

v0:
```python
import jax
import jax.numpy as jnp
from jax import lax
from jax.sharding import PartitionSpec as P

EXP_DEV = 2
BLOCKS = 8


def from_behind(block, axis, distance):
    devices = range(lax.axis_size(axis))
    route = [((i - distance) % len(devices), i) for i in devices]
    return lax.ppermute(block, axis, route)


def slot_products(hidden, grad_out, slot_of, block_live):
    block_total = slot_of.shape[0]
    rows_per = hidden.shape[0] // block_total
    results = []
    for slot in range(EXP_DEV + 1):
        chosen = (slot_of == slot) & block_live
        row_mask = jnp.repeat(chosen, rows_per).astype(hidden.dtype)
        masked = hidden * row_mask[:, None]
        results.append(
            lax.dot_general(
                masked, grad_out, (((0,), (0,)), ((), ())), preferred_element_type=jnp.float32
            )
        )
    return jnp.stack(results)


def pick(placement, device):
    return lax.dynamic_index_in_dim(placement, device, 0, keepdims=False)


def deliver(home_slots, received, expert, wanted):
    local_slot = expert % EXP_DEV
    weight = jnp.where(wanted & (jnp.arange(EXP_DEV) == local_slot), 1.0, 0.0).astype(jnp.float32)
    return home_slots + weight[:, None, None] * received[None]


def fold_replicas(home_slots, replica, placement, holder, holders):
    quarter = holders // 4
    for distance in range(1, 4):
        sender = (holder + distance * quarter) % holders
        received = from_behind(
            replica.astype(jnp.bfloat16), "expert", holders - distance * quarter
        ).astype(replica.dtype)
        expert = pick(placement, sender)
        home_slots = deliver(home_slots, received, expert, expert // EXP_DEV == holder)
    return home_slots


def body(hidden, grad_out, block_slot, block_count, replica_expert):
    holder = lax.axis_index("expert")
    holders = lax.axis_size("expert")
    places = jnp.arange(BLOCKS, dtype=jnp.int32)
    block_live = places < block_count[0]
    totals = slot_products(hidden, grad_out, block_slot[0], block_live)
    home_slots = fold_replicas(totals[:EXP_DEV], totals[EXP_DEV], replica_expert, holder, holders)
    shares = lax.psum_scatter(home_slots, "dp", scatter_dimension=2, tiled=True)
    return shares.astype(jnp.bfloat16)


def solution(mesh):
    in_specs = (
        P(("dp", "expert"), None),
        P(("dp", "expert"), None),
        P(("dp", "expert"), None),
        P(("dp", "expert")),
        P(),
    )
    out_specs = P("expert", None, "dp")
    return jax.shard_map(body, mesh=mesh, in_specs=in_specs, out_specs=out_specs, check_vma=False)
```

profile of v0, /device:TPU:4, one launch (start us, length us, event | category | flops | bytes accessed | tf_op | source)
XLA Modules:
  0.0 541.7 jit_solution(393946294411780110)
XLA Ops:
  6.5 0.0 reduce-scatter.2.cloned.1.call-start
  7.2 0.7 fusion.8
  7.9 0.1 broadcast_bitcast_fusion
  7.9 0.0 copy-start
  7.9 7.9 %convolution_convert_fusion = bf16[768,2048]{1,0:T(8,128)(2,1)} fusion(bf16[1024,2048]{1,0:T(8,128)(2,1)} %param.6, bf16[1024,768]{1,0:T(8,128)(2,1)} %param.5, bf16[1024]{0:T(1024)(128)(2,1)S(1)} %broadcast_bitcast_fusion), kind=kOutput, calls=%fused_computation.5 | convolution fusion | flops 3223584768 | bytes 8914944 | tf_op jit(solution)/shard_map/dot_general | solution.py:25
  15.8 3.2 collective-permute-start.2
  19.0 7.2 %collective-permute-start.1 = (bf16[768,2048]{1,0:T(8,128)(2,1)}, bf16[768,2048]{1,0:T(8,128)(2,1)S(1)}, u32[]{:S(2)}, u32[]{:S(2)}) collective-permute-start(bf16[768,2048]{1,0:T(8,128)(2,1)} %convolution_convert_fusion), channel_id=1, source_target_pairs={{32,0},{33,1},{34,2},{35,3},{36,4},{37,5},{38,6},{39,7},{40,8},{41... | collective-permute-start | bytes 9437192 | tf_op jit(solution)/shard_map/ppermute | solution.py:13
  26.2 5.1 collective-permute-start
  31.3 0.0 copy-done
  31.3 0.7 fusion.11
  39.6 0.1 broadcast_bitcast_fusion.1
  39.7 0.0 copy-start.1
  39.7 0.0 copy-start.2
  39.7 9.0 %convolution_bitcast_fusion = f32[1,768,2048]{2,1,0:T(8,128)} fusion(bf16[1024,2048]{1,0:T(8,128)(2,1)} %param.6, bf16[1024,768]{1,0:T(8,128)(2,1)} %param.5, bf16[1024]{0:T(1024)(128)(2,1)S(1)} %get-tuple-element.11), kind=kOutput, calls=%fused_computation.3 | convolution fusion | flops 3222011904 | bytes 12060672 | tf_op jit(solution)/shard_map/dot_general | solution.py:25
  48.7 0.0 copy-done.1
  48.7 0.0 copy-done.2
  48.7 5.6 %convolution_bitcast_fusion.1 = f32[1,768,2048]{2,1,0:T(8,128)} fusion(bf16[1024,2048]{1,0:T(8,128)(2,1)S(1)} %copy-done.1, bf16[1024,768]{1,0:T(8,128)(2,1)S(1)} %copy-done.2, bf16[1024]{0:T(1024)(128)(2,1)S(1)} %get-tuple-element.12), kind=kOutput, calls=%fused_computation.4 | convolution fusion | flops 3222011904 | bytes 12060672 | tf_op jit(solution)/shard_map/dot_general | solution.py:25
  54.3 76.7 %collective-permute-done.2 = bf16[768,2048]{1,0:T(8,128)(2,1)} collective-permute-done((bf16[768,2048]{1,0:T(8,128)(2,1)}, bf16[768,2048]{1,0:T(8,128)(2,1)}, u32[]{:S(2)}, u32[]{:S(2)}) %collective-permute-start.2) | collective-permute-done | bytes 3145760 | tf_op jit(solution)/shard_map/ppermute | solution.py:13
  131.0 2.7 convert_element_type.59
  133.7 0.0 collective-permute-done.1
  133.7 0.8 convert_element_type.58
  134.6 163.2 %collective-permute-done = bf16[768,2048]{1,0:T(8,128)(2,1)} collective-permute-done((bf16[768,2048]{1,0:T(8,128)(2,1)}, bf16[768,2048]{1,0:T(8,128)(2,1)}, u32[]{:S(2)}, u32[]{:S(2)}) %collective-permute-start) | collective-permute-done | bytes 3145760 | tf_op jit(solution)/shard_map/ppermute | solution.py:13
  297.8 2.7 convert_element_type.57
  300.5 11.9 %fusion.1 = f32[2,768,2048]{2,1,0:T(8,128)} fusion(f32[1,768,2048]{2,1,0:T(8,128)} %convolution_bitcast_fusion, f32[1,768,2048]{2,1,0:T(8,128)} %convolution_bitcast_fusion.1, f32[768,2048]{1,0:T(8,128)S(1)} %convert_element_type.59, f32[2]{0:T(128)S(1)} %get-tuple-element.13, f32[768,2048]{1,0:T(8,128)S(1)} %convert_element_type.58, ...), kind=kLoop, calls=%fused_computation.2 | loop fusion | flops 22020096 | bytes 44040216 | tf_op jit(solution)/shard_map/add | solution.py:39
  312.4 0.0 reduce-scatter.2.cloned.1.call-update
  312.5 219.1 %reduce-scatter.2.cloned.1.call-done = f32[2,768,512]{2,1,0:T(8,128)} async-done(((f32[2,768,2048]{2,1,0:T(8,128)}), f32[2,768,512]{2,1,0:T(8,128)}) %reduce-scatter.2.cloned.1.call-update) | async-done | bytes 3145744 | tf_op jit(solution)/shard_map/reduce_scatter | solution.py:61
  531.6 3.2 convert_element_type.60
  (2 shorter events, 0.0 us)
Async XLA Ops:
  6.5 525.1 %reduce-scatter.2.cloned.1.call-start = ((), (), s32[]{:S(2)}) async-start(), calls=%async_computation.1 | async-start | bytes 15728640 | tf_op jit(solution)/shard_map/reduce_scatter | solution.py:61
  7.9 23.4 %copy-start = (s32[64]{0:T(128)S(1)}, s32[64]{0:T(128)}, u32[]{:S(2)}) copy-start(s32[64]{0:T(128)} %param.9) | copy-start | bytes 772
  15.8 115.2 %collective-permute-start.2 = (bf16[768,2048]{1,0:T(8,128)(2,1)}, bf16[768,2048]{1,0:T(8,128)(2,1)}, u32[]{:S(2)}, u32[]{:S(2)}) collective-permute-start(bf16[768,2048]{1,0:T(8,128)(2,1)} %convolution_convert_fusion), channel_id=1, source_target_pairs={{48,0},{49,1},{50,2},{51,3},{52,4},{53,5},{54,6},{55,7},{56,8},{57... | collective-permute-start | bytes 9437192 | tf_op jit(solution)/shard_map/ppermute | solution.py:13
  19.0 114.7 %collective-permute-start.1 = (bf16[768,2048]{1,0:T(8,128)(2,1)}, bf16[768,2048]{1,0:T(8,128)(2,1)S(1)}, u32[]{:S(2)}, u32[]{:S(2)}) collective-permute-start(bf16[768,2048]{1,0:T(8,128)(2,1)} %convolution_convert_fusion), channel_id=1, source_target_pairs={{32,0},{33,1},{34,2},{35,3},{36,4},{37,5},{38,6},{39,7},{40,8},{41... | collective-permute-start | bytes 9437192 | tf_op jit(solution)/shard_map/ppermute | solution.py:13
  26.2 271.6 %collective-permute-start = (bf16[768,2048]{1,0:T(8,128)(2,1)}, bf16[768,2048]{1,0:T(8,128)(2,1)}, u32[]{:S(2)}, u32[]{:S(2)}) collective-permute-start(bf16[768,2048]{1,0:T(8,128)(2,1)} %convolution_convert_fusion), channel_id=1, source_target_pairs={{16,0},{17,1},{18,2},{19,3},{20,4},{21,5},{22,6},{23,7},{24,8},{25... | collective-permute-start | bytes 9437192 | tf_op jit(solution)/shard_map/ppermute | solution.py:13
  39.7 9.0 %copy-start.1 = (bf16[1024,2048]{1,0:T(8,128)(2,1)S(1)}, bf16[1024,2048]{1,0:T(8,128)(2,1)}, u32[]{:S(2)}) copy-start(bf16[1024,2048]{1,0:T(8,128)(2,1)} %param.6) | copy-start | bytes 12582916
  39.7 9.0 %copy-start.2 = (bf16[1024,768]{1,0:T(8,128)(2,1)S(1)}, bf16[1024,768]{1,0:T(8,128)(2,1)}, u32[]{:S(2)}) copy-start(bf16[1024,768]{1,0:T(8,128)(2,1)} %param.5) | copy-start | bytes 4718596
Sparse Core Ops, SparseCore 0:
  312.6 218.9 reduce-scatter.1
where the time goes:
time: 543 us; the launch traced here: 542 us
  waiting for transfers between devices  459 us (85%)
  matrix products  22.5 us (4%)
  other arithmetic  22.1 us (4%)
  between operations  21.7 us (4%)
  starting transfers between devices  15.5 us (3%)
    ppermute x3, waiting for transfers between devices, from_behind(): return lax.ppermute(block, axis, route)  240 us
    reduce_scatter x1, waiting for transfers between devices, body(): shares = lax.psum_scatter(home_slots, 'dp', scatter_dimension=2, tiled=True)  219 us
    dot_general x3, matrix products, slot_products(): lax.dot_general(masked, grad_out, (((0,), (0,)), ((), ())), preferred_ele...  22.5 us
    ppermute x3, starting transfers between devices, from_behind(): return lax.ppermute(block, axis, route)  15.5 us
    add x1, other arithmetic, deliver(): return home_slots + weight[:, None, None] * received[None]  11.9 us
  transfers between devices with their start and end apart: 4, of which 3 were waited for; matrix products, arithmetic and copies ran while one was open for 3% of the time, Pallas kernels for 0%

commit v1 on v0

v1 whole, which is shorter than its diff:
```python
import jax
import jax.numpy as jnp
from jax import lax
from jax.sharding import PartitionSpec as P

EXP_DEV = 2
BLOCKS = 8


def slot_products(hidden, grad_out, slot_of, block_live):
    rows_per = hidden.shape[0] // slot_of.shape[0]
    results = []
    for slot in range(EXP_DEV + 1):
        chosen = (slot_of == slot) & block_live
        row_mask = jnp.repeat(chosen, rows_per).astype(hidden.dtype)
        masked = hidden * row_mask[:, None]
        results.append(
            lax.dot_general(
                masked, grad_out, (((0,), (0,)), ((), ())), preferred_element_type=jnp.float32
            ).astype(jnp.bfloat16)
        )
    return jnp.stack(results)


def swap(block, distance):
    n = lax.axis_size("expert")
    return lax.ppermute(block, "expert", [(i, i ^ distance) for i in range(n)])


def body(hidden, grad_out, block_slot, block_count, replica_expert):
    me = lax.axis_index("expert")
    half = lax.axis_size("expert") // 2
    quarter = half // 2
    live = jnp.arange(BLOCKS, dtype=jnp.int32) < block_count[0]
    mine = replica_expert[me]
    slots = block_slot[0]
    own = (slots == EXP_DEV) & (mine // EXP_DEV == me)
    slots = jnp.where(own, mine % EXP_DEV, slots)
    totals = slot_products(hidden, grad_out, slots, live)
    shares = lax.psum_scatter(totals, "dp", scatter_dimension=2, tiled=True)
    replica = shares[EXP_DEV]
    side = swap(replica, quarter)
    side_expert = replica_expert[me ^ quarter]
    across = me ^ half
    out = jnp.where(mine // EXP_DEV == across, replica.astype(jnp.float32), 0.0) + jnp.where(
        side_expert // EXP_DEV == across, side.astype(jnp.float32), 0.0
    )
    came = swap(out.astype(jnp.bfloat16), half)
    came_expert = replica_expert[across]
    home = []
    for slot in range(EXP_DEV):
        total = shares[slot].astype(jnp.float32)
        total += jnp.where(side_expert == me * EXP_DEV + slot, side.astype(jnp.float32), 0.0)
        total += jnp.where(came_expert == me * EXP_DEV + slot, came.astype(jnp.float32), 0.0)
        home.append(total.astype(jnp.bfloat16))
    return jnp.stack(home)


def solution(mesh):
    in_specs = (
        P(("dp", "expert"), None),
        P(("dp", "expert"), None),
        P(("dp", "expert"), None),
        P(("dp", "expert")),
        P(),
    )
    out_specs = P("expert", None, "dp")
    return jax.shard_map(body, mesh=mesh, in_specs=in_specs, out_specs=out_specs, check_vma=False)
```

time: 543 us -> 274 us (0.50)
  waiting for transfers between devices: 459 us -> 216 us
  other arithmetic: 22.1 us -> 10.3 us
  matrix products: 22.5 us -> 14.2 us
  starting transfers between devices: 15.5 us -> 8.14 us
    ppermute x3 -> x2, waiting for transfers between devices: 240 us -> 46.1 us  [swap(): return lax.ppermute(block, 'expert', [(i, i ^ distance) for i in range(n)])]
    reduce_scatter x1, waiting for transfers between devices: 219 us -> 170 us  [body(): shares = lax.psum_scatter(totals, 'dp', scatter_dimension=2, tiled=True)]
    add x1 -> x0, other arithmetic: 11.9 us -> none  [deliver(): return home_slots + weight[:, None, None] * received[None]]
    dot_general x3, matrix products: 22.5 us -> 14.2 us  [slot_products(): lax.dot_general(masked, grad_out, (((0,), (0,)), ((), ())), preferred_ele...]
    ppermute x3 -> x2, starting transfers between devices: 15.5 us -> 8.14 us  [swap(): return lax.ppermute(block, 'expert', [(i, i ^ distance) for i in range(n)])]
    another operation x0 -> x3, other arithmetic: none -> 7.34 us  [the longest x1 4.27 us: slot_products(): return jnp.stack(results)]
    convert_element_type x4 -> x1, other arithmetic: 9.51 us -> 2.3 us  [body(): came = swap(out.astype(jnp.bfloat16), half)]
  transfers between devices with their start and end apart: 4 -> 3, of which waited for: 3 -> 3; matrix products, arithmetic and copies ran while one was open for 3% -> 0% of each run, Pallas kernels for 0% -> 0%
where the time goes in v1:
time: 274 us; the launch traced here: 273 us
  waiting for transfers between devices  216 us (79%)
  between operations  21.5 us (8%)
  matrix products  14.2 us (5%)
  other arithmetic  10.3 us (4%)
  starting transfers between devices  8.14 us (3%)
  local copies, waits for them, and re-layouts  3.64 us (1%)
    reduce_scatter x1, waiting for transfers between devices, body(): shares = lax.psum_scatter(totals, 'dp', scatter_dimension=2, tiled=True)  170 us
    ppermute x2, waiting for transfers between devices, swap(): return lax.ppermute(block, 'expert', [(i, i ^ distance) for i in range(n)])  46.1 us
    dot_general x3, matrix products, slot_products(): lax.dot_general(masked, grad_out, (((0,), (0,)), ((), ())), preferred_ele...  14.2 us
    ppermute x2, starting transfers between devices, swap(): return lax.ppermute(block, 'expert', [(i, i ^ distance) for i in range(n)])  8.14 us
  transfers between devices with their start and end apart: 3, of which 3 were waited for; matrix products, arithmetic and copies ran while one was open for 0% of the time, Pallas kernels for 0%

profile of v1, /device:TPU:4, one launch (start us, length us, event | category | flops | bytes accessed | tf_op | source)
XLA Modules:
  0.0 273.5 jit_solution(12651027634242136865)
XLA Ops:
  6.5 0.0 reduce-scatter.2.cloned.1.call-start
  6.5 1.4 fusion.19
  11.2 0.7 and_convert_fusion.2
  11.9 0.1 broadcast_bitcast_fusion
  12.0 0.0 copy-start.1
  12.0 0.0 copy-start.2
  12.0 6.4 %fusion.1 = bf16[1,768,2048]{2,1,0:T(8,128)(2,1)S(1)} fusion(bf16[1024,2048]{1,0:T(8,128)(2,1)} %param.6, bf16[1024,768]{1,0:T(8,128)(2,1)} %param.5, bf16[1024]{0:T(1024)(128)(2,1)S(1)} %get-tuple-element.15), kind=kOutput, calls=%fused_computation.5 | convolution fusion | flops 3223584768 | bytes 8914944 | tf_op jit(solution)/shard_map/dot_general | solution.py:18
  18.4 0.0 copy-done.1
  18.4 0.0 copy-done.2
  18.4 3.9 %fusion.2 = bf16[1,768,2048]{2,1,0:T(8,128)(2,1)S(1)} fusion(bf16[1024,2048]{1,0:T(8,128)(2,1)S(1)} %copy-done.1, bf16[1024,768]{1,0:T(8,128)(2,1)S(1)} %copy-done.2, bf16[1024]{0:T(1024)(128)(2,1)S(1)} %get-tuple-element.14), kind=kOutput, calls=%fused_computation.6 | convolution fusion | flops 3223584768 | bytes 8914944 | tf_op jit(solution)/shard_map/dot_general | solution.py:18
  22.3 0.1 broadcast_bitcast_fusion.2
  22.4 3.9 %fusion = bf16[1,768,2048]{2,1,0:T(8,128)(2,1)S(1)} fusion(bf16[1024,2048]{1,0:T(8,128)(2,1)S(1)} %copy-done.1, bf16[1024,768]{1,0:T(8,128)(2,1)S(1)} %copy-done.2, bf16[1024]{0:T(1024)(128)(2,1)S(1)} %broadcast_bitcast_fusion.2), kind=kOutput, calls=%fused_computation.4 | convolution fusion | flops 3223584768 | bytes 8914944 | tf_op jit(solution)/shard_map/dot_general | solution.py:18
  26.3 4.3 %pad_maximum_fusion = bf16[3,768,2048]{2,1,0:T(8,128)(2,1)} fusion(bf16[1,768,2048]{2,1,0:T(8,128)(2,1)S(1)} %fusion.2, bf16[1,768,2048]{2,1,0:T(8,128)(2,1)S(1)} %fusion.1, bf16[1,768,2048]{2,1,0:T(8,128)(2,1)S(1)} %fusion), kind=kLoop, calls=%fused_computation | loop fusion | flops 9437184 | bytes 18874368 | tf_op jit(solution)/shard_map/stack | solution.py:22
  30.6 0.0 reduce-scatter.2.cloned.1.call-update
  30.6 169.5 %reduce-scatter.2.cloned.1.call-done = bf16[3,768,512]{2,1,0:T(8,128)(2,1)} async-done(((bf16[3,768,2048]{2,1,0:T(8,128)(2,1)}), bf16[3,768,512]{2,1,0:T(8,128)(2,1)}) %reduce-scatter.2.cloned.1.call-update) | async-done | bytes 2359312 | tf_op jit(solution)/shard_map/reduce_scatter | solution.py:40
  200.2 2.1 slice_bitcast_fusion.1
  202.2 0.0 copy-start
  202.2 3.0 %collective-permute-start = (bf16[768,512]{1,0:T(8,128)(2,1)}, bf16[768,512]{1,0:T(8,128)(2,1)S(1)}, u32[]{:S(2)}, u32[]{:S(2)}) collective-permute-start(bf16[768,512]{1,0:T(8,128)(2,1)} %slice_bitcast_fusion.1), channel_id=1, source_target_pairs={{0,16},{1,17},{2,18},{3,19},{4,20},{5,21},{6,22},{7,23},{8,24},{9,... | collective-permute-start | bytes 2359304 | tf_op jit(solution)/shard_map/ppermute | solution.py:27
  207.5 15.3 %collective-permute-done = bf16[768,512]{1,0:T(8,128)(2,1)S(1)} collective-permute-done((bf16[768,512]{1,0:T(8,128)(2,1)}, bf16[768,512]{1,0:T(8,128)(2,1)S(1)}, u32[]{:S(2)}, u32[]{:S(2)}) %collective-permute-start) | collective-permute-done | bytes 786464 | tf_op jit(solution)/shard_map/ppermute | solution.py:27
  222.8 2.3 fusion.9
  225.1 5.1 %collective-permute-start.1 = (bf16[768,512]{1,0:T(8,128)(2,1)}, bf16[768,512]{1,0:T(8,128)(2,1)}, u32[]{:S(2)}, u32[]{:S(2)}) collective-permute-start(bf16[768,512]{1,0:T(8,128)(2,1)} %fusion.9), channel_id=1, source_target_pairs={{0,32},{1,33},{2,34},{3,35},{4,36},{5,37},{6,38},{7,39},{8,40},{9,... | collective-permute-start | bytes 2359304 | tf_op jit(solution)/shard_map/ppermute | solution.py:27
  232.7 30.8 %collective-permute-done.1 = bf16[768,512]{1,0:T(8,128)(2,1)} collective-permute-done((bf16[768,512]{1,0:T(8,128)(2,1)}, bf16[768,512]{1,0:T(8,128)(2,1)}, u32[]{:S(2)}, u32[]{:S(2)}) %collective-permute-start.1) | collective-permute-done | bytes 786464 | tf_op jit(solution)/shard_map/ppermute | solution.py:27
  263.5 0.0 copy-done
  263.5 1.8 fusion.15
  265.3 1.3 pad_maximum_fusion.1
  (1 shorter events, 0.0 us)
Async XLA Ops:
  6.5 193.6 %reduce-scatter.2.cloned.1.call-start = ((), (), s32[]{:S(2)}) async-start(), calls=%async_computation.1 | async-start | bytes 11796480 | tf_op jit(solution)/shard_map/reduce_scatter | solution.py:40
  12.0 6.4 %copy-start.1 = (bf16[1024,2048]{1,0:T(8,128)(2,1)S(1)}, bf16[1024,2048]{1,0:T(8,128)(2,1)}, u32[]{:S(2)}) copy-start(bf16[1024,2048]{1,0:T(8,128)(2,1)} %param.6) | copy-start | bytes 12582916
  12.0 6.4 %copy-start.2 = (bf16[1024,768]{1,0:T(8,128)(2,1)S(1)}, bf16[1024,768]{1,0:T(8,128)(2,1)}, u32[]{:S(2)}) copy-start(bf16[1024,768]{1,0:T(8,128)(2,1)} %param.5) | copy-start | bytes 4718596
  202.2 61.3 %copy-start = (bf16[3,768,512]{2,1,0:T(8,128)(2,1)S(1)}, bf16[3,768,512]{2,1,0:T(8,128)(2,1)}, u32[]{:S(2)}) copy-start(bf16[3,768,512]{2,1,0:T(8,128)(2,1)} %reduce-scatter.2.cloned.1.call-done) | copy-start | bytes 7077892
  202.2 20.6 %collective-permute-start = (bf16[768,512]{1,0:T(8,128)(2,1)}, bf16[768,512]{1,0:T(8,128)(2,1)S(1)}, u32[]{:S(2)}, u32[]{:S(2)}) collective-permute-start(bf16[768,512]{1,0:T(8,128)(2,1)} %slice_bitcast_fusion.1), channel_id=1, source_target_pairs={{0,16},{1,17},{2,18},{3,19},{4,20},{5,21},{6,22},{7,23},{8,24},{9,... | collective-permute-start | bytes 2359304 | tf_op jit(solution)/shard_map/ppermute | solution.py:27
  225.1 38.4 %collective-permute-start.1 = (bf16[768,512]{1,0:T(8,128)(2,1)}, bf16[768,512]{1,0:T(8,128)(2,1)}, u32[]{:S(2)}, u32[]{:S(2)}) collective-permute-start(bf16[768,512]{1,0:T(8,128)(2,1)} %fusion.9), channel_id=1, source_target_pairs={{0,32},{1,33},{2,34},{3,35},{4,36},{5,37},{6,38},{7,39},{8,40},{9,... | collective-permute-start | bytes 2359304 | tf_op jit(solution)/shard_map/ppermute | solution.py:27
Sparse Core Ops, SparseCore 0:
  30.7 169.3 reduce-scatter.1

commit v2 on v0

v2 whole, which is shorter than its diff:
```python
import functools

import jax
import jax.numpy as jnp
from jax import lax
from jax.experimental import pallas as pl
from jax.experimental.pallas import tpu as pltpu
from jax.sharding import PartitionSpec as P

EXP_DEV = 2
SUPER = 128
ROWS = 32
LAG = 2
OWN_LAG = 3
MESH = pl.DeviceIdType.MESH
F32 = jnp.float32
BF16 = jnp.bfloat16


def flag(condition):
    return jnp.where(condition, 1.0, 0.0).astype(F32)


def kernel(
    holders, slot_ref, count_ref, rep_ref, hid_ref, grad_ref, out_ref,
    lhs, home, rown, ra, rb, vs, vr, vx, hs, hr,
    y1_send, y2_send, v_send, h_send, ra_recv, rb_recv, vr_recv, vx_recv, hr_recv,
):
    lo = lax.axis_index("dp")
    me = lax.axis_index("expert")
    half = holders // 2
    quarter = holders // 4
    ystep = holders // 8
    hi = lax.div(me, half)
    ring = lax.rem(me, half)
    across = lax.rem(me + half, holders)
    side = hi * half + lax.rem(ring + quarter, half)
    upper = lax.div(lo, 2)
    outer = (lo == 0) | (lo == 3)
    inner = (lo == 1) | (lo == 2)

    tokens, ff = hid_ref.shape
    share = grad_ref.shape[1] // 4
    blocks = slot_ref.shape[0]
    block = tokens // blocks
    chunks = ff // ROWS
    per_super = SUPER // ROWS

    def y_target(n):
        step = ystep + lax.rem(n, 2) * (half - 2 * ystep)
        return hi * half + lax.rem(ring + step, half)

    barrier = pltpu.get_barrier_semaphore()
    up = (lax.rem(lo + 1, 4), lax.rem(me + lax.div(lo, 3) * half, holders))
    down = (lax.rem(lo + 3, 4), lax.rem(me + lax.div(3 - lo, 3) * half, holders))
    for target in (up, down, (lo, y_target(0)), (lo, y_target(1))):
        pl.semaphore_signal(barrier, inc=1, device_id=target, device_id_type=MESH)

    mine = rep_ref[me]
    beside = rep_ref[side]
    over = rep_ref[across]
    keep_own = flag(lax.div(mine, EXP_DEV) == across)
    keep_side = flag(lax.div(beside, EXP_DEV) == across)
    side_slot = [flag(beside == me * EXP_DEV + s) for s in range(EXP_DEV)]
    over_slot = [flag(over == me * EXP_DEV + s) for s in range(EXP_DEV)]
    home_here = lax.div(mine, EXP_DEV) == me
    weights = []
    for b in range(blocks):
        live = b < count_ref[0]
        slot = slot_ref[b]
        slot = jnp.where((slot == EXP_DEV) & home_here, lax.rem(mine, EXP_DEV), slot)
        weights.append([flag(live & (slot == s)) for s in range(EXP_DEV + 1)])

    def rows_of(c):
        return pl.ds(pl.multiple_of(c * ROWS, ROWS), ROWS)

    def outward(n):
        return n + upper * (3 - 2 * n)

    def swap_copy(c, n, src, dst, send_sem, recv_sem):
        j, rows = outward(n), rows_of(c)
        return pltpu.make_async_remote_copy(
            src_ref=src.at[j, rows], dst_ref=dst.at[j, rows],
            send_sem=send_sem, recv_sem=recv_sem.at[c, j],
            device_id=(lo, y_target(n)), device_id_type=MESH,
        )

    def first_swap(c, n):
        return swap_copy(c, n, rown, ra, y1_send, ra_recv)

    def second_swap(c, n):
        return swap_copy(c, n, ra, rb, y2_send, rb_recv)

    def to_outer(c, j):
        return pltpu.make_async_remote_copy(
            src_ref=vs.at[j, rows_of(c)], dst_ref=vr.at[j, rows_of(c)],
            send_sem=v_send, recv_sem=vr_recv.at[c, j],
            device_id=(3 * upper, me), device_id_type=MESH,
        )

    def to_across(c, j):
        return pltpu.make_async_remote_copy(
            src_ref=vs.at[j, rows_of(c)], dst_ref=vx.at[j, rows_of(c)],
            send_sem=v_send, recv_sem=vx_recv.at[c, j],
            device_id=(3 - lo, across), device_id_type=MESH,
        )

    def home_copy(c, j, place, target):
        return pltpu.make_async_remote_copy(
            src_ref=hs.at[j, :, rows_of(c)], dst_ref=hr.at[place, :, rows_of(c)],
            send_sem=h_send, recv_sem=hr_recv.at[c, place],
            device_id=(target, me), device_id_type=MESH,
        )

    def products(c):
        start = pl.multiple_of(c * ROWS, SUPER)
        lanes = pl.ds(start, SUPER)
        for b in range(blocks):
            turned = hid_ref[b * block:(b + 1) * block, lanes].astype(F32).T
            for s in range(EXP_DEV + 1):
                lhs[s * SUPER:(s + 1) * SUPER, b * block:(b + 1) * block] = (
                    turned * weights[b][s]
                ).astype(BF16)

        def one(n, carry):
            j = outward(n)
            columns = pl.ds(pl.multiple_of(j * share, share), share)
            made = jnp.dot(lhs[...], grad_ref[:, columns], preferred_element_type=F32)
            for s in range(EXP_DEV):
                home[j, s, lanes, :] = made[s * SUPER:(s + 1) * SUPER]
            rown[j, lanes, :] = made[EXP_DEV * SUPER:].astype(BF16)
            first_swap(c, n).start()
            return carry

        lax.fori_loop(0, 4, one, 0)

    def stage_a(c):
        @pl.when(lax.rem(c, per_super) == 0)
        def _():
            products(c)

        @pl.when(lax.rem(c, per_super) != 0)
        def _():
            def one(n, carry):
                first_swap(c, n).start()
                return carry

            lax.fori_loop(0, 4, one, 0)

    def stage_b(c):
        def one(n, carry):
            first_swap(c, n).wait_recv()
            second_swap(c, n).start()
            return carry

        lax.fori_loop(0, 4, one, 0)

    def stage_c(c):
        rows = rows_of(c)

        def one(n, carry):
            j = outward(n)
            second_swap(c, n).wait_recv()
            value = keep_own * rown[j, rows, :].astype(F32) + keep_side * rb[j, rows, :].astype(F32)

            @pl.when(inner)
            def _():
                vs[j, rows, :] = value.astype(BF16)
                to_outer(c, j).start()

            @pl.when(outer)
            def _():
                to_outer(c, j).wait_recv()
                vs[j, rows, :] = (value + vr[j, rows, :].astype(F32)).astype(BF16)
                to_across(c, j).start()

            return carry

        lax.fori_loop(0, 4, one, 0)

    def started(c, j, s):
        rows = rows_of(c)
        return home[j, s, rows, :] + side_slot[s] * rb[j, rows, :].astype(F32)

    def stage_d(c):
        rows = rows_of(c)

        def one(m, carry):
            last = lax.div(m, 2)
            j = (1 - last) * ((3 - m) - upper * (3 - 2 * m)) + last * (lo + 1 - 2 * lax.rem(lo, 2))

            @pl.when(outer)
            def _():
                to_across(c, j).wait_recv()
                for s in range(EXP_DEV):
                    hs[j, s, rows, :] = (
                        started(c, j, s) + over_slot[s] * vx[j, rows, :].astype(F32)
                    ).astype(BF16)

            @pl.when(inner)
            def _():
                home_copy(c, j, j, lax.rem(lo + 1, 4)).wait_recv()
                for s in range(EXP_DEV):
                    hs[j, s, rows, :] = (started(c, j, s) + hr[j, s, rows, :].astype(F32)).astype(BF16)

            @pl.when(j > lo)
            def _():
                home_copy(c, j, j, lax.rem(lo + 1, 4)).start()

            @pl.when(j == lo - 1)
            def _():
                home_copy(c, j, 4, lax.rem(lo + 3, 4)).start()

            @pl.when(j < lo - 1)
            def _():
                home_copy(c, j, j, lax.rem(lo + 3, 4)).start()

            return carry

        lax.fori_loop(0, 3, one, 0)

    def stage_e(c):
        rows = rows_of(c)

        @pl.when(outer)
        def _():
            place = 4 - lax.div(lo, 3)
            to_across(c, lo).wait_recv()
            home_copy(c, lo, place, lax.rem(lo + 1, 4)).wait_recv()
            for s in range(EXP_DEV):
                out_ref[s, rows, :] = (
                    started(c, lo, s)
                    + over_slot[s] * vx[lo, rows, :].astype(F32)
                    + hr[place, s, rows, :].astype(F32)
                ).astype(BF16)

        @pl.when(inner)
        def _():
            home_copy(c, lo, lo, lax.rem(lo + 1, 4)).wait_recv()
            home_copy(c, lo, 4, lax.rem(lo + 1, 4)).wait_recv()
            for s in range(EXP_DEV):
                out_ref[s, rows, :] = (
                    started(c, lo, s)
                    + hr[lo, s, rows, :].astype(F32)
                    + hr[4, s, rows, :].astype(F32)
                ).astype(BF16)

    def guarded(stage, c):
        @pl.when((c >= 0) & (c < chunks))
        def _():
            stage(c)

    pl.semaphore_wait(barrier, 4)
    extra = lax.div(3 - lo, 3) + lax.div(lo, 3)

    def tick(t, carry):
        guarded(stage_a, t)
        guarded(stage_b, t - 1)
        guarded(stage_c, t - 2 - extra)
        guarded(stage_d, t - 2 - LAG)
        guarded(stage_e, t - 2 - LAG - OWN_LAG)
        return carry

    lax.fori_loop(0, chunks + 2 + LAG + OWN_LAG, tick, 0)

    def drained(src, dst, sem):
        pltpu.make_async_remote_copy(
            src_ref=src, dst_ref=dst, send_sem=sem, recv_sem=vr_recv.at[0, 0],
            device_id=(lo, y_target(0)), device_id_type=MESH,
        ).wait_send()

    drained(rown, ra, y1_send)
    drained(ra, rb, y2_send)
    drained(vs, vr, v_send)
    drained(hs.at[0:3], hr.at[0:3], h_send)


def body(hidden, grad_out, block_slot, block_count, replica_expert):
    holders = lax.axis_size("expert")
    ff, width = hidden.shape[1], grad_out.shape[1]
    share = width // 4
    chunks = ff // ROWS
    column = (4, ff, share)
    dma = pltpu.SemaphoreType.DMA
    smem = pl.BlockSpec(memory_space=pltpu.SMEM)
    vmem = pl.BlockSpec(memory_space=pltpu.VMEM)
    return pl.pallas_call(
        functools.partial(kernel, holders),
        out_shape=jax.ShapeDtypeStruct((EXP_DEV, ff, share), BF16),
        in_specs=[smem, smem, smem, vmem, vmem],
        out_specs=vmem,
        scratch_shapes=[
            pltpu.VMEM(((EXP_DEV + 1) * SUPER, hidden.shape[0]), BF16),
            pltpu.VMEM((4, EXP_DEV, ff, share), F32),
            pltpu.VMEM(column, BF16),
            pltpu.VMEM(column, BF16),
            pltpu.VMEM(column, BF16),
            pltpu.VMEM(column, BF16),
            pltpu.VMEM(column, BF16),
            pltpu.VMEM(column, BF16),
            pltpu.VMEM((4, EXP_DEV, ff, share), BF16),
            pltpu.VMEM((5, EXP_DEV, ff, share), BF16),
            dma, dma, dma, dma,
            dma((chunks, 4)), dma((chunks, 4)), dma((chunks, 4)), dma((chunks, 4)), dma((chunks, 5)),
        ],
        compiler_params=pltpu.CompilerParams(
            collective_id=0, has_side_effects=True, vmem_limit_bytes=60 * 1024 * 1024
        ),
    )(block_slot[0], block_count, replica_expert, hidden, grad_out)


def solution(mesh):
    in_specs = (
        P(("dp", "expert"), None),
        P(("dp", "expert"), None),
        P(("dp", "expert"), None),
        P(("dp", "expert")),
        P(),
    )
    out_specs = P("expert", None, "dp")
    return jax.shard_map(body, mesh=mesh, in_specs=in_specs, out_specs=out_specs, check_vma=False)
```

time: 543 us -> 193 us (0.36)
  waiting for transfers between devices: 459 us -> 0 us
  Pallas kernels: 0 us -> 190 us
  matrix products: 22.5 us -> 0 us
  other arithmetic: 22.1 us -> 0 us
  between operations: 21.7 us -> 0.66 us
  starting transfers between devices: 15.5 us -> 0 us
    ppermute x3 -> x0, waiting for transfers between devices: 240 us -> none  [from_behind(): return lax.ppermute(block, axis, route)]
    reduce_scatter x1 -> x0, waiting for transfers between devices: 219 us -> none  [body(): shares = lax.psum_scatter(home_slots, 'dp', scatter_dimension=2, tiled=True)]
    pallas_call x0 -> x1, Pallas kernels: none -> 190 us  [body(): pl.pallas_call(functools.partial(kernel, holders), out_shape=jax.ShapeDty...]
    dot_general x3 -> x0, matrix products: 22.5 us -> none  [slot_products(): lax.dot_general(masked, grad_out, (((0,), (0,)), ((), ())), preferred_ele...]
    ppermute x3 -> x0, starting transfers between devices: 15.5 us -> none  [from_behind(): return lax.ppermute(block, axis, route)]
    add x1 -> x0, other arithmetic: 11.9 us -> none  [deliver(): return home_slots + weight[:, None, None] * received[None]]
    convert_element_type x5 -> x0, other arithmetic: 10.2 us -> none  [the longest x3 6.28 us: fold_replicas(): received = from_behind(replica.astype(jnp.bfloat16), 'expert', holders -...]
  transfers between devices with their start and end apart: 4 -> 0, of which waited for: 3 -> 0; matrix products, arithmetic and copies ran while one was open for 3% -> 0% of each run, Pallas kernels for 0% -> 0%
where the time goes in v2:
time: 193 us
  Pallas kernels  190 us (98%)
  local copies, waits for them, and re-layouts  2.65 us (1%)
    pallas_call x1, Pallas kernels, body(): pl.pallas_call(functools.partial(kernel, holders), out_shape=jax.ShapeDty...  190 us

profile of v2, /device:TPU:4, one launch (start us, length us, event | category | flops | bytes accessed | tf_op | source)
XLA Modules:
  0.0 193.2 jit_solution(2503057303791691258)
XLA Ops:
  0.7 189.9 %shard_map.55 = bf16[2,768,512]{2,1,0:T(8,128)(2,1)} custom-call(s32[8]{0:T(128)} %bitcast.1, s32[1]{0:T(128)S(6)} %copy.7.count_ref, s32[64]{0:T(128)} %rep_ref.1, bf16[1024,768]{1,0:T(8,128)(2,1)} %hid_ref.1, bf16[1024,2048]{1,0:T(8,128)(2,1)} %grad_ref.1), custom_call_target="tpu_custom_call" | custom-call | tf_op jit(solution)/shard_map/pallas_call | solution.py:287
  190.6 2.7 %copy.8 = bf16[2,768,512]{2,1,0:T(8,128)(2,1)} copy(bf16[2,768,512]{2,1,0:T(8,128)(2,1)} %shard_map.55) | data formatting | bytes 3145728

commit v3 on v2

v3 whole, which is shorter than its diff:
```python
import functools

import jax
import jax.numpy as jnp
from jax import lax
from jax.experimental import pallas as pl
from jax.experimental.pallas import tpu as pltpu
from jax.sharding import PartitionSpec as P

EXP_DEV = 2
SUPER = 128
ROWS = 64
EARLY = 2
LAGS = {
    "T": (-1, -1),
    "A": (0, 0),
    "H": (1, 1),
    "C": (1, 1),
    "D": (1, 4),
    "G": (2, 6),
    "F": (4, 6),
    "E": (7, 11),
}
MESH = pl.DeviceIdType.MESH
F32 = jnp.float32
BF16 = jnp.bfloat16


def flag(condition):
    return jnp.where(condition, 1.0, 0.0).astype(F32)


def kernel(
    holders, slot_ref, count_ref, rep_ref, hid_hbm, grad_hbm, out_hbm,
    hid, grad, out, lhs, home, rown, rb, vs, vr, vx, hs, hr, zs, hz,
    in_sem, out_sem, y_send, v_send, h_send, z_send,
    rb_recv, vr_recv, vx_recv, hr_recv, z_recv,
):
    lo = lax.axis_index("dp")
    me = lax.axis_index("expert")
    half = holders // 2
    quarter = holders // 4
    hi = lax.div(me, half)
    across = lax.rem(me + half, holders)
    side = hi * half + lax.rem(lax.rem(me, half) + quarter, half)
    upper = lax.div(lo, 2)
    outer = (lo == 0) | (lo == 3)
    inner = (lo == 1) | (lo == 2)
    at_end = lax.div(3 - lo, 3) + lax.div(lo, 3)

    tokens, ff = hid.shape
    share = grad.shape[1] // 4
    blocks = slot_ref.shape[0]
    block = tokens // blocks
    chunks = ff // ROWS
    per_super = SUPER // ROWS

    barrier = pltpu.get_barrier_semaphore()
    up = (lax.rem(lo + 1, 4), lax.rem(me + lax.div(lo, 3) * half, holders))
    down = (lax.rem(lo + 3, 4), lax.rem(me + lax.div(3 - lo, 3) * half, holders))
    for target in (up, down, (lo, side)):
        pl.semaphore_signal(barrier, inc=1, device_id=target, device_id_type=MESH)

    def outward(n):
        return n + upper * (3 - 2 * n)

    def hidden_part(part):
        lanes = (slice(0, SUPER), slice(SUPER, ff))[part]
        return pltpu.make_async_copy(hid_hbm.at[:, lanes], hid.at[:, lanes], in_sem.at[4 + part])

    def columns_of(j):
        return pl.ds(pl.multiple_of(j * share, share), share)

    def grad_part(j):
        return pltpu.make_async_copy(
            grad_hbm.at[:, columns_of(j)], grad.at[:, columns_of(j)], in_sem.at[j]
        )

    hidden_part(0).start()
    for n in range(4):
        grad_part(outward(n)).start()
    if ff > SUPER:
        hidden_part(1).start()

    mine = rep_ref[me]
    beside = rep_ref[side]
    over = rep_ref[across]
    keep_own = flag(lax.div(mine, EXP_DEV) == across)
    keep_side = flag(lax.div(beside, EXP_DEV) == across)
    side_slot = [flag(beside == me * EXP_DEV + s) for s in range(EXP_DEV)]
    over_slot = [flag(over == me * EXP_DEV + s) for s in range(EXP_DEV)]
    late_slot = [jnp.maximum(side_slot[s], over_slot[s]) for s in range(EXP_DEV)]
    home_here = lax.div(mine, EXP_DEV) == me
    weights = []
    for b in range(blocks):
        live = b < count_ref[0]
        slot = slot_ref[b]
        slot = jnp.where((slot == EXP_DEV) & home_here, lax.rem(mine, EXP_DEV), slot)
        weights.append([flag(live & (slot == s)) for s in range(EXP_DEV + 1)])

    def rows_of(c):
        return pl.ds(pl.multiple_of(c * ROWS, ROWS), ROWS)

    def swap(c, j):
        return pltpu.make_async_remote_copy(
            src_ref=rown.at[j, rows_of(c)], dst_ref=rb.at[j, rows_of(c)],
            send_sem=y_send, recv_sem=rb_recv.at[c, j],
            device_id=(lo, side), device_id_type=MESH,
        )

    def to_outer(c, j):
        return pltpu.make_async_remote_copy(
            src_ref=vs.at[j, rows_of(c)], dst_ref=vr.at[j, rows_of(c)],
            send_sem=v_send, recv_sem=vr_recv.at[c, j],
            device_id=(3 * upper, me), device_id_type=MESH,
        )

    def to_across(c, j):
        return pltpu.make_async_remote_copy(
            src_ref=vs.at[j, rows_of(c)], dst_ref=vx.at[j, rows_of(c)],
            send_sem=v_send, recv_sem=vx_recv.at[c, j],
            device_id=(3 - lo, across), device_id_type=MESH,
        )

    def home_copy(c, j, place, target):
        return pltpu.make_async_remote_copy(
            src_ref=hs.at[j, :, rows_of(c)], dst_ref=hr.at[place, :, rows_of(c)],
            send_sem=h_send, recv_sem=hr_recv.at[c, place],
            device_id=(target, me), device_id_type=MESH,
        )

    def arrived(c, place):
        home_copy(c, 0, place, lax.rem(lo + 1, 4)).wait_recv()

    def late_copy(c, j):
        return pltpu.make_async_remote_copy(
            src_ref=zs.at[j, rows_of(c)], dst_ref=hz.at[j, rows_of(c)],
            send_sem=z_send, recv_sem=z_recv.at[c, j],
            device_id=(1 + upper, me), device_id_type=MESH,
        )

    def send_home(c, j):
        @pl.when(j > lo)
        def _():
            home_copy(c, j, j, lax.rem(lo + 1, 4)).start()

        @pl.when(j == lo - 1)
        def _():
            home_copy(c, j, 4, lax.rem(lo + 3, 4)).start()

        @pl.when(j < lo - 1)
        def _():
            home_copy(c, j, j, lax.rem(lo + 3, 4)).start()

    def side_of(c):
        return lax.rem(lax.div(c, per_super), 2)

    def turn(c):
        lanes = pl.ds(pl.multiple_of(c * ROWS, SUPER), SUPER)
        for b in range(blocks):
            turned = hid[b * block:(b + 1) * block, lanes].astype(F32).T
            for s in range(EXP_DEV + 1):
                lhs[side_of(c), s * SUPER:(s + 1) * SUPER, b * block:(b + 1) * block] = (
                    turned * weights[b][s]
                ).astype(BF16)

    def stage_t(c):
        @pl.when((c > 0) & (lax.rem(c, per_super) == 0))
        def _():
            @pl.when(c == per_super)
            def _():
                hidden_part(1).wait()

            turn(c)

    def stage_a(c):
        def one(n, carry):
            j = outward(n)

            @pl.when(lax.rem(c, per_super) == 0)
            def _():
                @pl.when(c == 0)
                def _():
                    grad_part(j).wait()

                lanes = pl.ds(pl.multiple_of(c * ROWS, SUPER), SUPER)
                made = jnp.dot(
                    lhs[side_of(c), EXP_DEV * SUPER:, :], grad[:, columns_of(j)],
                    preferred_element_type=F32,
                )
                rown[j, lanes, :] = made.astype(BF16)

            swap(c, j).start()
            return carry

        lax.fori_loop(0, 4, one, 0)

    def stage_h(c):
        @pl.when(lax.rem(c, per_super) == 0)
        def _():
            lanes = pl.ds(pl.multiple_of(c * ROWS, SUPER), SUPER)

            def one(n, carry):
                j = outward(3 - n)
                made = jnp.dot(
                    lhs[side_of(c), :EXP_DEV * SUPER, :], grad[:, columns_of(j)],
                    preferred_element_type=F32,
                )
                for s in range(EXP_DEV):
                    home[j, s, lanes, :] = made[s * SUPER:(s + 1) * SUPER]
                if EARLY:
                    @pl.when((c == 0) & outer & (n < 3))
                    def _():
                        for q in range(EARLY):
                            for s in range(EXP_DEV):
                                hs[j, s, rows_of(q), :] = home[j, s, rows_of(q), :].astype(BF16)
                            send_home(q, j)
                return carry

            lax.fori_loop(0, 4, one, 0)

    def stage_c(c):
        rows = rows_of(c)

        def one(n, carry):
            j = outward(n)
            swap(c, j).wait_recv()
            value = keep_own * rown[j, rows, :].astype(F32) + keep_side * rb[j, rows, :].astype(F32)

            @pl.when(inner)
            def _():
                vs[j, rows, :] = value.astype(BF16)
                to_outer(c, j).start()

            @pl.when(outer)
            def _():
                to_outer(c, j).wait_recv()
                vs[j, rows, :] = (value + vr[j, rows, :].astype(F32)).astype(BF16)
                to_across(c, j).start()

            return carry

        lax.fori_loop(0, 4, one, 0)

    def started(c, j, s):
        rows = rows_of(c)
        return home[j, s, rows, :] + side_slot[s] * rb[j, rows, :].astype(F32)

    def home_sum(c, m):
        rows = rows_of(c)
        j = (3 - m) - upper * (3 - 2 * m) if m < 2 else lo + 1 - 2 * lax.rem(lo, 2)

        @pl.when(outer)
        def _():
            to_across(c, j).wait_recv()

            @pl.when(c < EARLY)
            def _():
                zs[j, rows, :] = (
                    (side_slot[0] + side_slot[1]) * rb[j, rows, :].astype(F32)
                    + (over_slot[0] + over_slot[1]) * vx[j, rows, :].astype(F32)
                ).astype(BF16)
                late_copy(c, j).start()

            @pl.when(c >= EARLY)
            def _():
                for s in range(EXP_DEV):
                    hs[j, s, rows, :] = (
                        started(c, j, s) + over_slot[s] * vx[j, rows, :].astype(F32)
                    ).astype(BF16)
                send_home(c, j)

        @pl.when(inner)
        def _():
            arrived(c, j)

            def passed(extra):
                for s in range(EXP_DEV):
                    hs[j, s, rows, :] = (
                        started(c, j, s) + hr[j, s, rows, :].astype(F32) + extra(s)
                    ).astype(BF16)

            if m < 2 and EARLY:
                @pl.when(c < EARLY)
                def _():
                    late_copy(c, j).wait_recv()
                    passed(lambda s: late_slot[s] * hz[j, rows, :].astype(F32))

                @pl.when(c >= EARLY)
                def _():
                    passed(lambda s: 0.0)
            else:
                passed(lambda s: 0.0)
            send_home(c, j)

    def stage_d(c):
        home_sum(c, 0)

    def stage_g(c):
        home_sum(c, 1)

    def stage_f(c):
        home_sum(c, 2)

    def stage_e(c):
        rows = rows_of(c)

        @pl.when(outer)
        def _():
            place = 4 - lax.div(lo, 3)
            to_across(c, lo).wait_recv()
            arrived(c, place)
            for s in range(EXP_DEV):
                out[s, rows, :] = (
                    started(c, lo, s)
                    + over_slot[s] * vx[lo, rows, :].astype(F32)
                    + hr[place, s, rows, :].astype(F32)
                ).astype(BF16)

        @pl.when(inner)
        def _():
            arrived(c, lo)
            arrived(c, 4)

            def summed(extra):
                for s in range(EXP_DEV):
                    out[s, rows, :] = (
                        started(c, lo, s)
                        + hr[lo, s, rows, :].astype(F32)
                        + hr[4, s, rows, :].astype(F32)
                        + extra(s)
                    ).astype(BF16)

            if EARLY:
                @pl.when(c < EARLY)
                def _():
                    late_copy(c, lo).wait_recv()
                    summed(lambda s: late_slot[s] * hz[lo, rows, :].astype(F32))

                @pl.when(c >= EARLY)
                def _():
                    summed(lambda s: 0.0)
            else:
                summed(lambda s: 0.0)

        pltpu.make_async_copy(out.at[:, rows], out_hbm.at[:, rows], out_sem).start()

    hidden_part(0).wait()
    turn(0)
    pl.semaphore_wait(barrier, 3)

    def tick(t, carry):
        def guarded(stage, name):
            at, between = LAGS[name]
            c = t - between - at_end * (at - between)

            @pl.when((c >= 0) & (c < chunks))
            def _():
                stage(c)

        guarded(stage_f, "F")
        guarded(stage_a, "A")
        guarded(stage_h, "H")
        guarded(stage_c, "C")
        guarded(stage_g, "G")
        guarded(stage_t, "T")
        guarded(stage_d, "D")
        guarded(stage_e, "E")
        return carry

    lax.fori_loop(0, chunks + max(max(lags) for lags in LAGS.values()), tick, 0)

    def drained(src, dst, sem):
        pltpu.make_async_remote_copy(
            src_ref=src, dst_ref=dst, send_sem=sem, recv_sem=vr_recv.at[0, 0],
            device_id=(lo, side), device_id_type=MESH,
        ).wait_send()

    drained(rown, rb, y_send)
    drained(vs, vr, v_send)
    drained(hs.at[0:3], hr.at[0:3], h_send)
    if EARLY:
        @pl.when(outer)
        def _():
            drained(zs.at[0:3], hz.at[0:3], z_send)
    pltpu.make_async_copy(out, out_hbm, out_sem).wait()


def body(hidden, grad_out, block_slot, block_count, replica_expert):
    holders = lax.axis_size("expert")
    ff, width = hidden.shape[1], grad_out.shape[1]
    share = width // 4
    chunks = ff // ROWS
    column = (4, ff, share)
    early = (4, max(EARLY, 1) * ROWS, share)
    dma = pltpu.SemaphoreType.DMA
    smem = pl.BlockSpec(memory_space=pltpu.SMEM)
    hbm = pl.BlockSpec(memory_space=pl.ANY)
    return pl.pallas_call(
        functools.partial(kernel, holders),
        out_shape=jax.ShapeDtypeStruct((EXP_DEV, ff, share), BF16),
        in_specs=[smem, smem, smem, hbm, hbm],
        out_specs=hbm,
        scratch_shapes=[
            pltpu.VMEM(hidden.shape, BF16),
            pltpu.VMEM(grad_out.shape, BF16),
            pltpu.VMEM((EXP_DEV, ff, share), BF16),
            pltpu.VMEM((2, (EXP_DEV + 1) * SUPER, hidden.shape[0]), BF16),
            pltpu.VMEM((4, EXP_DEV, ff, share), F32),
            pltpu.VMEM(column, BF16),
            pltpu.VMEM(column, BF16),
            pltpu.VMEM(column, BF16),
            pltpu.VMEM(column, BF16),
            pltpu.VMEM(column, BF16),
            pltpu.VMEM((4, EXP_DEV, ff, share), BF16),
            pltpu.VMEM((5, EXP_DEV, ff, share), BF16),
            pltpu.VMEM(early, BF16),
            pltpu.VMEM(early, BF16),
            dma((6,)), dma, dma, dma, dma, dma,
            dma((chunks, 4)), dma((chunks, 4)), dma((chunks, 4)), dma((chunks, 5)),
            dma((max(EARLY, 1), 4)),
        ],
        compiler_params=pltpu.CompilerParams(
            collective_id=0, has_side_effects=True, vmem_limit_bytes=60 * 1024 * 1024
        ),
    )(block_slot[0], block_count, replica_expert, hidden, grad_out)


def solution(mesh):
    in_specs = (
        P(("dp", "expert"), None),
        P(("dp", "expert"), None),
        P(("dp", "expert"), None),
        P(("dp", "expert")),
        P(),
    )
    out_specs = P("expert", None, "dp")
    return jax.shard_map(body, mesh=mesh, in_specs=in_specs, out_specs=out_specs, check_vma=False)
```

time: 193 us -> 126 us (0.65)
  Pallas kernels: 190 us -> 122 us
    pallas_call x1, Pallas kernels: 190 us -> 122 us  [body(): pl.pallas_call(functools.partial(kernel, holders), out_shape=jax.ShapeDty...]
where the time goes in v3:
time: 126 us
  Pallas kernels  122 us (97%)
  local copies, waits for them, and re-layouts  2.65 us (2%)
    pallas_call x1, Pallas kernels, body(): pl.pallas_call(functools.partial(kernel, holders), out_shape=jax.ShapeDty...  122 us
    unnamed x1, local copies, waits for them, and re-layouts  2.65 us

profile of v3, /device:TPU:4, one launch (start us, length us, event | category | flops | bytes accessed | tf_op | source)
XLA Modules:
  0.0 125.5 jit_solution(10892761867524947025)
XLA Ops:
  0.7 122.2 %shard_map.55 = bf16[2,768,512]{2,1,0:T(8,128)(2,1)} custom-call(s32[8]{0:T(128)} %bitcast.1, s32[1]{0:T(128)S(6)} %copy.7.count_ref, s32[64]{0:T(128)} %rep_ref.1, bf16[1024,768]{1,0:T(8,128)(2,1)} %hid_hbm.1, bf16[1024,2048]{1,0:T(8,128)(2,1)} %grad_hbm.1), custom_call_target="tpu_custom_call" | custom-call | tf_op jit(solution)/shard_map/pallas_call | solution.py:399
  122.8 2.7 %copy.8 = bf16[2,768,512]{2,1,0:T(8,128)(2,1)} copy(bf16[2,768,512]{2,1,0:T(8,128)(2,1)} %shard_map.55) | data formatting | bytes 3145728

commit v4 on v3

--- a/solution.py
+++ b/solution.py
@@ -10,16 +10,16 @@
 EXP_DEV = 2
 SUPER = 128
 ROWS = 64
-EARLY = 2
+EARLY = 6
 LAGS = {
     "T": (-1, -1),
     "A": (0, 0),
     "H": (1, 1),
-    "C": (1, 1),
-    "D": (1, 4),
-    "G": (2, 6),
-    "F": (4, 6),
-    "E": (7, 11),
+    "C": (3, 1),
+    "D": (3, 4),
+    "G": (4, 6),
+    "F": (6, 6),
+    "E": (11, 10),
 }
 MESH = pl.DeviceIdType.MESH
 F32 = jnp.float32
@@ -31,9 +31,9 @@
 
 
 def kernel(
-    holders, slot_ref, count_ref, rep_ref, hid_hbm, grad_hbm, out_hbm,
-    hid, grad, out, lhs, home, rown, rb, vs, vr, vx, hs, hr, zs, hz,
-    in_sem, out_sem, y_send, v_send, h_send, z_send,
+    holders, slot_hbm, count_hbm, rep_hbm, hid_hbm, grad_hbm, out_hbm,
+    slot_ref, count_ref, rep_ref, hid, grad, out, lhs, home, rown, rb, vs, vr, vx, hs, hr, zs, hz,
+    int_sem, in_sem, out_sem, y_send, v_send, h_send, z_send,
     rb_recv, vr_recv, vx_recv, hr_recv, z_recv,
 ):
     lo = lax.axis_index("dp")
@@ -76,12 +76,22 @@
             grad_hbm.at[:, columns_of(j)], grad.at[:, columns_of(j)], in_sem.at[j]
         )
 
+    small = [
+        pltpu.make_async_copy(src, dst, int_sem.at[k])
+        for k, (src, dst) in enumerate(
+            ((slot_hbm, slot_ref), (count_hbm, count_ref), (rep_hbm, rep_ref))
+        )
+    ]
+    for copy in small:
+        copy.start()
     hidden_part(0).start()
     for n in range(4):
-        grad_part(outward(n)).start()
+        grad_part(outward(n + at_end * (3 - 2 * n) if EARLY else n)).start()
     if ff > SUPER:
         hidden_part(1).start()
 
+    for copy in small:
+        copy.wait()
     mine = rep_ref[me]
     beside = rep_ref[side]
     over = rep_ref[across]
@@ -132,10 +142,10 @@
     def arrived(c, place):
         home_copy(c, 0, place, lax.rem(lo + 1, 4)).wait_recv()
 
-    def late_copy(c, j):
+    def late_copy(i):
         return pltpu.make_async_remote_copy(
-            src_ref=zs.at[j, rows_of(c)], dst_ref=hz.at[j, rows_of(c)],
-            send_sem=z_send, recv_sem=z_recv.at[c, j],
+            src_ref=zs.at[i], dst_ref=hz.at[i],
+            send_sem=z_send, recv_sem=z_recv.at[i],
             device_id=(1 + upper, me), device_id_type=MESH,
         )
 
@@ -179,7 +189,7 @@
 
             @pl.when(lax.rem(c, per_super) == 0)
             def _():
-                @pl.when(c == 0)
+                @pl.when((c == 0) & inner if EARLY else c == 0)
                 def _():
                     grad_part(j).wait()
 
@@ -196,28 +206,38 @@
         lax.fori_loop(0, 4, one, 0)
 
     def stage_h(c):
-        @pl.when(lax.rem(c, per_super) == 0)
-        def _():
-            lanes = pl.ds(pl.multiple_of(c * ROWS, SUPER), SUPER)
-
-            def one(n, carry):
-                j = outward(3 - n)
-                made = jnp.dot(
-                    lhs[side_of(c), :EXP_DEV * SUPER, :], grad[:, columns_of(j)],
-                    preferred_element_type=F32,
-                )
-                for s in range(EXP_DEV):
-                    home[j, s, lanes, :] = made[s * SUPER:(s + 1) * SUPER]
-                if EARLY:
-                    @pl.when((c == 0) & outer & (n < 3))
-                    def _():
-                        for q in range(EARLY):
+        @pl.when((lax.rem(c, per_super) == 0) & ((c > 0) | inner) if EARLY else lax.rem(c, per_super) == 0)
+        def _():
+            home_products(c)
+
+    def home_products(c):
+        lanes = pl.ds(pl.multiple_of(c * ROWS, SUPER), SUPER)
+
+        def one(n, carry):
+            j = outward(3 - n)
+            if EARLY:
+                @pl.when((c == 0) & outer)
+                def _():
+                    grad_part(j).wait()
+
+            made = jnp.dot(
+                lhs[side_of(c), :EXP_DEV * SUPER, :], grad[:, columns_of(j)],
+                preferred_element_type=F32,
+            )
+            for s in range(EXP_DEV):
+                home[j, s, lanes, :] = made[s * SUPER:(s + 1) * SUPER]
+            if EARLY:
+                @pl.when((c == 0) & outer & (n < 3))
+                def _():
+                    for q in range(pl.cdiv(EARLY, 3)):
+                        @pl.when(3 * q + n < EARLY)
+                        def _(q=q):
                             for s in range(EXP_DEV):
                                 hs[j, s, rows_of(q), :] = home[j, s, rows_of(q), :].astype(BF16)
                             send_home(q, j)
-                return carry
-
-            lax.fori_loop(0, 4, one, 0)
+            return carry
+
+        lax.fori_loop(0, 4, one, 0)
 
     def stage_c(c):
         rows = rows_of(c)
@@ -254,15 +274,16 @@
         def _():
             to_across(c, j).wait_recv()
 
-            @pl.when(c < EARLY)
-            def _():
-                zs[j, rows, :] = (
+            @pl.when(3 * c + m < EARLY)
+            def _():
+                i = lax.rem(3 * c + m, max(EARLY, 1))
+                zs[i] = (
                     (side_slot[0] + side_slot[1]) * rb[j, rows, :].astype(F32)
                     + (over_slot[0] + over_slot[1]) * vx[j, rows, :].astype(F32)
                 ).astype(BF16)
-                late_copy(c, j).start()
-
-            @pl.when(c >= EARLY)
+                late_copy(i).start()
+
+            @pl.when(3 * c + m >= EARLY)
             def _():
                 for s in range(EXP_DEV):
                     hs[j, s, rows, :] = (
@@ -281,12 +302,13 @@
                     ).astype(BF16)
 
             if m < 2 and EARLY:
-                @pl.when(c < EARLY)
-                def _():
-                    late_copy(c, j).wait_recv()
-                    passed(lambda s: late_slot[s] * hz[j, rows, :].astype(F32))
-
-                @pl.when(c >= EARLY)
+                @pl.when(3 * c + m < EARLY)
+                def _():
+                    i = lax.rem(3 * c + m, EARLY)
+                    late_copy(i).wait_recv()
+                    passed(lambda s: late_slot[s] * hz[i].astype(F32))
+
+                @pl.when(3 * c + m >= EARLY)
                 def _():
                     passed(lambda s: 0.0)
             else:
@@ -332,12 +354,13 @@
                     ).astype(BF16)
 
             if EARLY:
-                @pl.when(c < EARLY)
-                def _():
-                    late_copy(c, lo).wait_recv()
-                    summed(lambda s: late_slot[s] * hz[lo, rows, :].astype(F32))
-
-                @pl.when(c >= EARLY)
+                @pl.when(3 * c + 2 < EARLY)
+                def _():
+                    i = lax.rem(3 * c + 2, EARLY)
+                    late_copy(i).wait_recv()
+                    summed(lambda s: late_slot[s] * hz[i].astype(F32))
+
+                @pl.when(3 * c + 2 >= EARLY)
                 def _():
                     summed(lambda s: 0.0)
             else:
@@ -348,6 +371,10 @@
     hidden_part(0).wait()
     turn(0)
     pl.semaphore_wait(barrier, 3)
+    if EARLY:
+        @pl.when(outer)
+        def _():
+            home_products(jnp.int32(0))
 
     def tick(t, carry):
         def guarded(stage, name):
@@ -358,14 +385,14 @@
             def _():
                 stage(c)
 
+        guarded(stage_h, "H")
+        guarded(stage_a, "A")
         guarded(stage_f, "F")
-        guarded(stage_a, "A")
-        guarded(stage_h, "H")
+        guarded(stage_g, "G")
         guarded(stage_c, "C")
-        guarded(stage_g, "G")
+        guarded(stage_e, "E")
+        guarded(stage_d, "D")
         guarded(stage_t, "T")
-        guarded(stage_d, "D")
-        guarded(stage_e, "E")
         return carry
 
     lax.fori_loop(0, chunks + max(max(lags) for lags in LAGS.values()), tick, 0)
@@ -382,7 +409,7 @@
     if EARLY:
         @pl.when(outer)
         def _():
-            drained(zs.at[0:3], hz.at[0:3], z_send)
+            drained(zs, hz, z_send)
     pltpu.make_async_copy(out, out_hbm, out_sem).wait()
 
 
@@ -392,16 +419,18 @@
     share = width // 4
     chunks = ff // ROWS
     column = (4, ff, share)
-    early = (4, max(EARLY, 1) * ROWS, share)
+    early = (max(EARLY, 1), ROWS, share)
     dma = pltpu.SemaphoreType.DMA
-    smem = pl.BlockSpec(memory_space=pltpu.SMEM)
-    hbm = pl.BlockSpec(memory_space=pl.ANY)
+    fixed = pl.BlockSpec(memory_space=pltpu.HBM)
     return pl.pallas_call(
         functools.partial(kernel, holders),
         out_shape=jax.ShapeDtypeStruct((EXP_DEV, ff, share), BF16),
-        in_specs=[smem, smem, smem, hbm, hbm],
-        out_specs=hbm,
+        in_specs=[fixed] * 5,
+        out_specs=pl.BlockSpec(memory_space=pl.ANY),
         scratch_shapes=[
+            pltpu.SMEM((block_slot.shape[1],), jnp.int32),
+            pltpu.SMEM(block_count.shape, jnp.int32),
+            pltpu.SMEM(replica_expert.shape, jnp.int32),
             pltpu.VMEM(hidden.shape, BF16),
             pltpu.VMEM(grad_out.shape, BF16),
             pltpu.VMEM((EXP_DEV, ff, share), BF16),
@@ -416,14 +445,17 @@
             pltpu.VMEM((5, EXP_DEV, ff, share), BF16),
             pltpu.VMEM(early, BF16),
             pltpu.VMEM(early, BF16),
-            dma((6,)), dma, dma, dma, dma, dma,
+            dma((3,)), dma((6,)), dma, dma, dma, dma, dma,
             dma((chunks, 4)), dma((chunks, 4)), dma((chunks, 4)), dma((chunks, 5)),
-            dma((max(EARLY, 1), 4)),
+            dma((max(EARLY, 1),)),
         ],
         compiler_params=pltpu.CompilerParams(
-            collective_id=0, has_side_effects=True, vmem_limit_bytes=60 * 1024 * 1024
+            collective_id=0, has_side_effects=True, vmem_limit_bytes=52 * 1024 * 1024
         ),
-    )(block_slot[0], block_count, replica_expert, hidden, grad_out)
+    )(
+        pltpu.with_memory_space_constraint(block_slot[0], pltpu.HBM), block_count,
+        pltpu.with_memory_space_constraint(replica_expert, pltpu.HBM), hidden, grad_out,
+    )
 
 
 def solution(mesh):

time: 126 us -> 123 us (0.976)
  local copies, waits for them, and re-layouts: 2.65 us -> 1.15 us
    pallas_call x1, Pallas kernels: 122 us -> 121 us  [body(): pl.pallas_call(functools.partial(kernel, holders), out_shape=jax.ShapeDty...]
    unnamed x1, local copies, waits for them, and re-layouts: 2.65 us -> 1.15 us
where the time goes in v4:
time: 123 us; the launch traced here: 122 us
  Pallas kernels  121 us (98%)
    pallas_call x1, Pallas kernels, body(): pl.pallas_call(functools.partial(kernel, holders), out_shape=jax.ShapeDty...  121 us

profile of v4, /device:TPU:4, one launch (start us, length us, event | category | flops | bytes accessed | tf_op | source)
XLA Modules:
  0.0 122.4 jit_solution(12310197570832833382)
XLA Ops:
  0.7 120.6 %shard_map.55 = bf16[2,768,512]{2,1,0:T(8,128)(2,1)S(1)} custom-call(s32[8]{0:T(128)} %bitcast.1, s32[1]{0:T(128)S(6)} %copy.7.count_hbm, s32[64]{0:T(128)} %rep_hbm.1, bf16[1024,768]{1,0:T(8,128)(2,1)} %hid_hbm.1, bf16[1024,2048]{1,0:T(8,128)(2,1)} %grad_hbm.1), custom_call_target="tpu_custom_call" | custom-call | tf_op jit(solution)/shard_map/pallas_call | solution.py:425
  121.3 1.1 copy.8

commit v5 on v4

--- a/solution.py
+++ b/solution.py
@@ -10,16 +10,17 @@
 EXP_DEV = 2
 SUPER = 128
 ROWS = 64
-EARLY = 6
+EARLY = 5
+SWITCH = 8
 LAGS = {
-    "T": (-1, -1),
-    "A": (0, 0),
-    "H": (1, 1),
-    "C": (3, 1),
-    "D": (3, 4),
-    "G": (4, 6),
-    "F": (6, 6),
-    "E": (11, 10),
+    "T": (-1, -1, 0, 0),
+    "A": (0, 0, 0, 0),
+    "H": (0, 0, 0, 0),
+    "C": (1, 1, 0, 0),
+    "D": (1, 5, 0, 0),
+    "G": (2, 5, 0, 4),
+    "F": (2, 9, 4, 0),
+    "E": (14, 13, 4, 1),
 }
 MESH = pl.DeviceIdType.MESH
 F32 = jnp.float32
@@ -84,11 +85,11 @@
     ]
     for copy in small:
         copy.start()
+    def needed(n):
+        return outward(n + at_end * (3 - 2 * n) if EARLY else n)
+
     hidden_part(0).start()
-    for n in range(4):
-        grad_part(outward(n + at_end * (3 - 2 * n) if EARLY else n)).start()
-    if ff > SUPER:
-        hidden_part(1).start()
+    grad_part(needed(0)).start()
 
     for copy in small:
         copy.wait()
@@ -369,6 +370,10 @@
         pltpu.make_async_copy(out.at[:, rows], out_hbm.at[:, rows], out_sem).start()
 
     hidden_part(0).wait()
+    for n in range(1, 4):
+        grad_part(needed(n)).start()
+    if ff > SUPER:
+        hidden_part(1).start()
     turn(0)
     pl.semaphore_wait(barrier, 3)
     if EARLY:
@@ -376,26 +381,31 @@
         def _():
             home_products(jnp.int32(0))
 
-    def tick(t, carry):
+    def tick(first, t, carry):
         def guarded(stage, name):
-            at, between = LAGS[name]
-            c = t - between - at_end * (at - between)
-
-            @pl.when((c >= 0) & (c < chunks))
+            at, between, at_more, between_more = LAGS[name]
+            lag = between + at_end * (at - between)
+            more = between_more + at_end * (at_more - between_more)
+            c = t - lag if first else t - lag - more
+            start = 0 if first else SWITCH - lag
+
+            @pl.when((c >= 0) & (c >= start) & (c < chunks))
             def _():
                 stage(c)
 
-        guarded(stage_h, "H")
         guarded(stage_a, "A")
+        guarded(stage_g, "G")
         guarded(stage_f, "F")
-        guarded(stage_g, "G")
+        guarded(stage_e, "E")
         guarded(stage_c, "C")
-        guarded(stage_e, "E")
         guarded(stage_d, "D")
         guarded(stage_t, "T")
+        guarded(stage_h, "H")
         return carry
 
-    lax.fori_loop(0, chunks + max(max(lags) for lags in LAGS.values()), tick, 0)
+    ticks = chunks + max(max(lags[0] + lags[2], lags[1] + lags[3]) for lags in LAGS.values())
+    lax.fori_loop(0, SWITCH, functools.partial(tick, True), 0)
+    lax.fori_loop(SWITCH, ticks, functools.partial(tick, False), 0)
 
     def drained(src, dst, sem):
         pltpu.make_async_remote_copy(

time: 123 us -> 121 us (0.984)
  Pallas kernels: 121 us -> 118 us
    pallas_call x1, Pallas kernels: 121 us -> 118 us  [body(): pl.pallas_call(functools.partial(kernel, holders), out_shape=jax.ShapeDty...]
where the time goes in v5:
time: 121 us; the launch traced here: 120 us
  Pallas kernels  118 us (98%)
    pallas_call x1, Pallas kernels, body(): pl.pallas_call(functools.partial(kernel, holders), out_shape=jax.ShapeDty...  118 us

profile of v5, /device:TPU:4, one launch (start us, length us, event | category | flops | bytes accessed | tf_op | source)
XLA Modules:
  0.0 119.8 jit_solution(6735530610602549430)
XLA Ops:
  0.7 118.0 %shard_map.55 = bf16[2,768,512]{2,1,0:T(8,128)(2,1)S(1)} custom-call(s32[8]{0:T(128)} %bitcast.1, s32[1]{0:T(128)S(6)} %copy.7.count_hbm, s32[64]{0:T(128)} %rep_hbm.1, bf16[1024,768]{1,0:T(8,128)(2,1)} %hid_hbm.1, bf16[1024,2048]{1,0:T(8,128)(2,1)} %grad_hbm.1), custom_call_target="tpu_custom_call" | custom-call | tf_op jit(solution)/shard_map/pallas_call | solution.py:435
  118.6 1.1 copy.8

commit v6 on v5

--- a/solution.py
+++ b/solution.py
@@ -18,9 +18,9 @@
     "H": (0, 0, 0, 0),
     "C": (1, 1, 0, 0),
     "D": (1, 5, 0, 0),
-    "G": (2, 5, 0, 4),
-    "F": (2, 9, 4, 0),
-    "E": (14, 13, 4, 1),
+    "G": (2, 5, 0, 3),
+    "F": (2, 8, 3, 0),
+    "E": (12, 12, 2, 1),
 }
 MESH = pl.DeviceIdType.MESH
 F32 = jnp.float32
@@ -85,11 +85,11 @@
     ]
     for copy in small:
         copy.start()
-    def needed(n):
-        return outward(n + at_end * (3 - 2 * n) if EARLY else n)
-
     hidden_part(0).start()
-    grad_part(needed(0)).start()
+    for n in range(4):
+        grad_part(outward(n + at_end * (3 - 2 * n) if EARLY else n)).start()
+    if ff > SUPER:
+        hidden_part(1).start()
 
     for copy in small:
         copy.wait()
@@ -370,10 +370,6 @@
         pltpu.make_async_copy(out.at[:, rows], out_hbm.at[:, rows], out_sem).start()
 
     hidden_part(0).wait()
-    for n in range(1, 4):
-        grad_part(needed(n)).start()
-    if ff > SUPER:
-        hidden_part(1).start()
     turn(0)
     pl.semaphore_wait(barrier, 3)
     if EARLY:

time: 121 us -> 120 us (level)
  no operation moved by 1% of the time
where the time goes in v6:
time: 120 us; the launch traced here: 119 us
  Pallas kernels  118 us (98%)
    pallas_call x1, Pallas kernels, body(): pl.pallas_call(functools.partial(kernel, holders), out_shape=jax.ShapeDty...  118 us

profile of v6, /device:TPU:4, one launch (start us, length us, event | category | flops | bytes accessed | tf_op | source)
XLA Modules:
  0.0 119.5 jit_solution(18000285047345739653)
XLA Ops:
  0.7 117.7 %shard_map.55 = bf16[2,768,512]{2,1,0:T(8,128)(2,1)S(1)} custom-call(s32[8]{0:T(128)} %bitcast.1, s32[1]{0:T(128)S(6)} %copy.7.count_hbm, s32[64]{0:T(128)} %rep_hbm.1, bf16[1024,768]{1,0:T(8,128)(2,1)} %hid_hbm.1, bf16[1024,2048]{1,0:T(8,128)(2,1)} %grad_hbm.1), custom_call_target="tpu_custom_call" | custom-call | tf_op jit(solution)/shard_map/pallas_call | solution.py:431
  118.3 1.1 copy.8
